TPU v7x, 256 devices: a whole 4x4x8 slice. The times are simulated.
256 devices in a mesh: dp: 64 (over z, x, core), rep: 4 (over y).
Axes of the slice: x: 4, y: 4, z: 8, core: 2. Of those that a mesh axis runs over, the one named last changes fastest.
Arguments:
- ecg: bfloat16 [4, 327680], P('rep', 'dp'), may hold values from -6 to 6
- conv_first: bfloat16 [5, 256], replicated, may hold values from -2.5 to 2.5
- conv_second: bfloat16 [512, 256], replicated, may hold values from -0.25 to 0.25
- conv_third: bfloat16 [512, 256], replicated, may hold values from -0.25 to 0.25
- enc_gain: float32 [256], replicated, may hold values from 0.1 to 1.9
- ctx_weight: bfloat16 [2, 512, 256], replicated, may hold values from -0.25 to 0.25
- head_weight: bfloat16 [256, 12, 256], replicated, may hold values from -0.375 to 0.375
- sources: int32 [4, 512, 4, 2], P('rep', 'dp'), may hold values from 0 to 63, as said below
Outputs:
- target_grad: float32 [4, 16384, 256], P('rep', 'dp')
- head_grad: float32 [4, 256, 12, 256], P('rep')
Inputs may be any that keep to these rules, and one draw needn't show every extreme that they name: sources[r, i, s] = (o, b): o is the piece index along the recording, b a block of 128 rows of that piece's 256 positions. Among the 32 entries of one piece at most 2 name the same piece o, and in every draw one piece o is named exactly 2 times by every piece of its recording.
All inputs are finite; a program needn't handle non-finite values.
Results may differ from a plain program's by a relative error of at most 0.0085.
Values may be sent and summed in bfloat16 or wider, within the bound.
No kernel may reach another device: no remote copies, remote signals or barrier semaphores. Data moves between devices by JAX's collectives and lax.ppermute only.
A program may use at most 128 MiB of HBM per device.

v0:
```python
import math
import jax
import jax.numpy as jnp
from jax import lax
from jax.sharding import PartitionSpec as P


def gelu_exact(values):
    return jax.nn.gelu(values, approximate=False)


def encode(piece, conv_first, conv_second, conv_third, enc_gain, ctx_weight):
    channels = conv_first.shape[1]
    positions = piece.shape[0] // 20
    frames = piece.reshape(4 * positions, 5)
    hidden_one = gelu_exact(jnp.dot(frames, conv_first, preferred_element_type=jnp.float32)).astype(
        jnp.bfloat16
    )
    hidden_two = gelu_exact(
        jnp.dot(
            hidden_one.reshape(2 * positions, 2 * channels),
            conv_second,
            preferred_element_type=jnp.float32,
        )
    ).astype(jnp.bfloat16)
    mixed = jnp.dot(
        hidden_two.reshape(positions, 2 * channels), conv_third, preferred_element_type=jnp.float32
    )
    average = jnp.mean(mixed, -1, keepdims=True)
    centred = mixed - average
    variance = jnp.mean(centred * centred, -1, keepdims=True)
    latent = (centred / jnp.sqrt(variance + 1e-05) * enc_gain).astype(jnp.bfloat16)
    latent_wide = latent.astype(jnp.float32)
    target = (
        latent_wide / jnp.sqrt(jnp.sum(latent_wide * latent_wide, -1, keepdims=True) + 1e-06)
    ).astype(jnp.bfloat16)
    context = latent
    for layer_index in range(ctx_weight.shape[0]):
        dilation = 2**layer_index
        before = jnp.concatenate(
            [jnp.zeros((dilation, channels), jnp.bfloat16), context[: positions - dilation]], 0
        )
        joined = jnp.concatenate([context, before], 1)
        update = gelu_exact(
            jnp.dot(joined, ctx_weight[layer_index], preferred_element_type=jnp.float32)
        )
        context = (context.astype(jnp.float32) + update).astype(jnp.bfloat16)
    return (target, context)


def score_piece(target, context, head_weight, negatives):
    positions, channels = target.shape
    horizon = head_weight.shape[1]
    groups = negatives.shape[0]
    pred = jnp.dot(
        context,
        head_weight.reshape(channels, horizon * channels),
        preferred_element_type=jnp.float32,
    ).reshape(positions, horizon, channels)
    pred_norm = jnp.sqrt(jnp.sum(pred * pred, -1, keepdims=True) + 1e-06)
    unit_pred = pred / pred_norm
    queries = unit_pred.astype(jnp.bfloat16)
    shifted = jnp.stack(
        [
            jnp.concatenate(
                [target[step_index + 1 :], jnp.zeros((step_index + 1, channels), jnp.bfloat16)], 0
            )
            for step_index in range(horizon)
        ],
        1,
    )
    usable = (
        lax.broadcasted_iota(jnp.int32, (positions, horizon), 0)
        + lax.broadcasted_iota(jnp.int32, (positions, horizon), 1)
        + 1
        < positions
    ).astype(jnp.float32)
    positive = 10.0 * jnp.sum(queries.astype(jnp.float32) * shifted.astype(jnp.float32), -1)
    grouped = queries.reshape(groups, -1, channels)
    negative = 10.0 * jnp.einsum(
        "gqc,gnc->gqn", grouped, negatives, preferred_element_type=jnp.float32
    )
    pos_exp = jnp.exp(positive)
    neg_exp = jnp.exp(negative)
    partition = pos_exp.reshape(groups, -1) + jnp.sum(neg_exp, -1)
    usable_grouped = usable.reshape(groups, -1)
    pos_weight = 10.0 * usable * (pos_exp / partition.reshape(positions, horizon) - 1.0)
    neg_weight = (10.0 * usable_grouped[:, :, None] * neg_exp / partition[:, :, None]).astype(
        jnp.bfloat16
    )
    neg_part = jnp.einsum("gqn,gnc->gqc", neg_weight, negatives, preferred_element_type=jnp.float32)
    query_grad = pos_weight[:, :, None] * shifted.astype(jnp.float32) + neg_part.reshape(
        positions, horizon, channels
    )
    neg_grad = jnp.einsum(
        "gqn,gqc->gnc", neg_weight, grouped, preferred_element_type=jnp.float32
    ).astype(jnp.bfloat16)
    pos_terms = pos_weight[:, :, None] * queries.astype(jnp.float32)
    pos_grad = jnp.zeros((positions, channels), jnp.float32)
    for step_index in range(horizon):
        moved = jnp.concatenate(
            [
                jnp.zeros((step_index + 1, channels), jnp.float32),
                pos_terms[: positions - step_index - 1, step_index],
            ],
            0,
        )
        pos_grad = pos_grad + moved
    radial = jnp.sum(unit_pred * query_grad, -1, keepdims=True)
    pred_grad = (
        ((query_grad - unit_pred * radial) / pred_norm)
        .astype(jnp.bfloat16)
        .reshape(positions, horizon * channels)
    )
    head_part = lax.dot_general(
        context, pred_grad, (((0,), (0,)), ((), ())), preferred_element_type=jnp.float32
    )
    return (pos_grad, neg_grad, head_part)


def local(ecg, conv_first, conv_second, conv_third, enc_gain, ctx_weight, head_weight, sources):
    owner_total = lax.axis_size("dp")
    groups = sources.shape[1]
    entries = sources.reshape(-1, 2)
    owner_id = entries[:, 0]
    block_id = entries[:, 1]
    entry_count = entries.shape[0]
    capacity = max(2, 2 * entry_count // owner_total)
    slot_total = owner_total * capacity
    earlier = lax.broadcasted_iota(jnp.int32, (entry_count, entry_count), 1) < lax.broadcasted_iota(
        jnp.int32, (entry_count, entry_count), 0
    )
    same_owner = owner_id[:, None] == owner_id[None, :]
    rank_of = jnp.sum((earlier & same_owner).astype(jnp.int32), 1)
    slot_of = owner_id * capacity + rank_of
    matches = slot_of[:, None] == jnp.arange(slot_total, dtype=jnp.int32)[None, :]
    wanted = jnp.sum(jnp.where(matches, block_id[:, None], 0), 0).reshape(owner_total, capacity)
    occupied = jnp.any(matches, 0)
    entry_of = jnp.sum(jnp.where(matches, jnp.arange(entry_count, dtype=jnp.int32)[:, None], 0), 0)
    requested = lax.all_to_all(wanted, "dp", split_axis=0, concat_axis=0, tiled=True)
    target, context = encode(
        ecg.reshape(-1), conv_first, conv_second, conv_third, enc_gain, ctx_weight
    )
    positions, channels = target.shape
    segment = lax.all_gather(target, "dp", axis=0, tiled=True)
    piece_count = segment.shape[0] // positions
    segment_blocks = segment.reshape(piece_count, positions // 128, 128, channels)
    chosen = jnp.take_along_axis(segment_blocks, wanted[:, :, None, None], axis=1)
    chosen = chosen.reshape(piece_count * capacity, 128, channels)
    fetched = jnp.take(chosen, slot_of, axis=0)
    negatives = fetched.reshape(groups, -1, channels)
    pos_grad, neg_grad, head_part = score_piece(target, context, head_weight, negatives)
    horizon = head_weight.shape[1]
    neg_blocks = neg_grad.reshape(entry_count, 128, channels)
    picked = jnp.take(neg_blocks, entry_of, axis=0)
    outgoing = jnp.where(occupied[:, None, None], picked, jnp.zeros_like(picked)).reshape(
        owner_total, capacity, 128, channels
    )
    returned = lax.all_to_all(outgoing, "dp", split_axis=0, concat_axis=0, tiled=True).reshape(
        slot_total, 128 * channels
    )
    placed = (
        requested.reshape(-1)[None, :] == jnp.arange(positions // 128, dtype=jnp.int32)[:, None]
    ).astype(jnp.bfloat16)
    summed = jnp.dot(placed, returned, preferred_element_type=jnp.float32).reshape(
        positions, channels
    )
    target_grad = ((pos_grad + summed) / horizon)[None]
    head_total = lax.psum(head_part, "dp")
    factor = math.sqrt(channels / (lax.axis_size("dp") * positions))
    head_grad = (head_total * factor).reshape(1, channels, horizon, channels)
    return (target_grad, head_grad)


def solution(mesh):
    in_specs = (P("rep", "dp"), P(), P(), P(), P(), P(), P(), P("rep", "dp", None, None))
    out_specs = (P("rep", "dp", None), P("rep", None, None, None))
    return jax.shard_map(local, mesh=mesh, in_specs=in_specs, out_specs=out_specs, check_vma=False)
```

profile of v0, /device:TPU:8, one launch (start us, length us, event | category | flops | bytes accessed | tf_op | source)
XLA Modules:
  0.0 485.1 jit_solution(15221614664519750533)
XLA Ops:
  7.2 0.8 reduce
  8.5 3.1 fusion.12
  11.8 1.3 fusion.22
  13.9 0.8 fusion.34
  15.3 0.7 all_to_all.9
  16.0 12.7 %all-to-all-start = ((s32[64,1,2]{2,1,0:T(1,128)}), s32[64,1,2]{2,1,0:T(1,128)}, u32[]{:S(2)}, u32[]{:S(2)}) async-start(s32[64,1,2]{2,1,0:T(1,128)} %bitcast.38), calls=%async_computation | async-start | bytes 65536 | tf_op jit(solution)/shard_map/all_to_all | solution.py:140
  28.8 1.6 slice.139
  30.4 1.6 slice.138
  32.0 1.6 slice.137
  33.6 1.6 slice.136
  35.2 1.6 slice.135
  36.7 0.9 slice.134
  37.7 1.6 slice.133
  39.3 1.6 slice.132
  40.8 1.6 slice.131
  42.4 1.6 slice.130
  44.0 1.6 slice.129
  47.1 0.8 broadcast_in_dim.116
  48.0 0.7 reduce_sum.109
  49.8 0.9 bitcast_dynamic-update-slice_fusion.11
  50.7 0.9 bitcast_dynamic-update-slice_fusion.10
  51.7 0.9 bitcast_dynamic-update-slice_fusion.9
  52.6 0.9 bitcast_dynamic-update-slice_fusion.8
  53.5 0.9 bitcast_dynamic-update-slice_fusion.7
  54.4 0.9 bitcast_dynamic-update-slice_fusion.6
  55.4 0.9 bitcast_dynamic-update-slice_fusion.4
  56.3 0.9 bitcast_dynamic-update-slice_fusion.3
  57.2 0.9 bitcast_dynamic-update-slice_fusion.2
  58.1 0.9 bitcast_dynamic-update-slice_fusion.1
  59.1 1.9 fusion.32
  61.0 0.7 fusion.40
  62.5 1.2 fusion.2
  64.2 1.2 copy-done.6
  65.4 2.3 copy.45
  67.7 2.5 reshape.248
  70.4 30.4 %all-gather.2.cloned.1.call-done = bf16[16384,256]{1,0:T(8,128)(2,1)} async-done(((bf16[256,256]{1,0:T(8,128)(2,1)}), bf16[16384,256]{1,0:T(8,128)(2,1)}) %all-gather.2.cloned.1.call-update) | async-done | bytes 8388624 | tf_op jit(solution)/shard_map/all_gather | solution.py:145
  100.8 10.6 %gather_fusion.2 = bf16[128,128,256]{2,1,0:T(8,128)(2,1)} fusion(bf16[64,2,128,256]{3,2,1,0:T(8,128)(2,1)} %bitcast.130, s32[128]{0:T(128)S(1)} %reshape.273), kind=kCustom, calls=%fused_computation.2 | custom fusion | bytes 16778240 | tf_op jit(solution)/shard_map/jit(take_along_axis)/gather | solution.py:148
  111.3 7.4 %broadcast_select_fusion = bf16[128,128,256]{2,1,0:T(8,128)(2,1)} fusion(bf16[128,128,256]{2,1,0:T(8,128)(2,1)} %gather_fusion.2, pred[128]{0:T(512)(128)(4,1)S(1)} %compare_and_fusion.1), kind=kLoop, calls=%fused_computation.5 | loop fusion | flops 4194304 | bytes 16777344 | tf_op jit(solution)/shard_map/jit(take_along_axis)/select_n | solution.py:148
  118.8 5.4 %gather_fusion = bf16[32,128,256]{2,1,0:T(8,128)(2,1)} fusion(bf16[128,128,256]{2,1,0:T(8,128)(2,1)} %broadcast_select_fusion, s32[1024]{0:T(1024)S(1)} %get-tuple-element.29), kind=kCustom, calls=%fused_computation | custom fusion | bytes 4194432 | tf_op jit(solution)/shard_map/jit(_take)/gather | solution.py:150
  124.1 1.9 bitcast_select_fusion
  126.1 3.8 fusion.1
  130.4 3.8 divide_convert_fusion
  134.3 1.4 convolution_convert_fusion
  135.9 6.4 %gather_fusion.1 = bf16[128,128,256]{2,1,0:T(8,128)(2,1)} fusion(bf16[32,128,256]{2,1,0:T(8,128)(2,1)S(1)} %bitcast.125, s32[1024]{0:T(1024)S(1)} %get-tuple-element.28), kind=kCustom, calls=%fused_computation.1 | custom fusion | bytes 16777728 | tf_op jit(solution)/shard_map/jit(_take)/gather | solution.py:155
  142.3 7.4 %select_select_fusion = bf16[64,2,128,256]{3,2,1,0:T(8,128)(2,1)} fusion(bf16[64,2,128,256]{3,2,1,0:T(8,128)(2,1)} %bitcast.126, pred[64,2]{1,0:T(8,128)(4,1)S(1)} %compare_and_fusion, pred[64,2]{1,0:T(8,128)(4,1)S(1)} %copy-done.27), kind=kLoop, calls=%fused_computation.4 | loop fusion | flops 8388608 | bytes 16777472 | tf_op jit(solution)/shard_map/jit(_where)/select_n | solution.py:156
  149.7 6.9 %all-to-all-start.1 = ((bf16[64,2,128,256]{3,2,1,0:T(8,128)(2,1)}), bf16[64,2,128,256]{3,2,1,0:T(8,128)(2,1)}, u32[]{:S(2)}, u32[]{:S(2)}) async-start(bf16[64,2,128,256]{3,2,1,0:T(8,128)(2,1)} %select_select_fusion), calls=%async_computation.1 | async-start | bytes 16777216 | tf_op jit(solution)/shard_map/all_to_all | solution.py:159
  157.2 1.5 reduce.8
  158.8 4.2 fusion.105
  163.0 4.8 reshape.254
  167.8 21.8 %divide_convert_fusion.1 = bf16[256,12,256]{2,0,1:T(8,128)(2,1)} fusion(f32[256,12]{0,1:T(8,128)S(1)} %add_sqrt_fusion, f32[256,12,256]{2,1,0:T(8,128)} %reshape.254, bf16[256,12,256]{2,0,1:T(8,128)(2,1)} %copy-done.12, f32[256,12]{0,1:T(8,128)S(1)} %get-tuple-element.18, f32[256,12,256]{2,0,1:T(8,128)S(1)} %copy-done.11), kind=kOutput, calls=%fused_computation.14 | output fusion | flops 10226943 | bytes 9461760 | tf_op jit(solution)/shard_map/mul | solution.py:111
  189.7 1.7 copy.53
  191.4 2.3 fusion.106
  194.2 0.7 slice_bitcast_fusion.7
  195.6 0.7 slice_bitcast_fusion.9
  196.4 0.7 slice_bitcast_fusion.10
  199.3 0.7 slice_bitcast_fusion.2
  200.0 0.7 slice_bitcast_fusion.3
  202.8 247.4 %all-reduce.28.cloned.1.call-done = f32[256,3072]{1,0:T(8,128)} async-done(((f32[256,3072]{1,0:T(8,128)}), f32[256,3072]{1,0:T(8,128)}) %all-reduce.28.cloned.1.call-update) | async-done | bytes 3145744 | tf_op jit(solution)/shard_map/psum | solution.py:169
  450.3 2.1 broadcast_multiply_fusion
  452.4 2.3 copy.54
  454.7 3.7 copy.55
  458.5 12.3 %copy.58 = bf16[16,8,128,256]{3,1,2,0:T(8,128)(2,1)} copy(bf16[16,8,128,256]{3,2,1,0:T(8,128)(2,1)} %bitcast.52) | data formatting | bytes 16777216
  470.9 4.7 fusion.90
  476.0 2.1 multiply_bitcast_fusion
  (137 shorter events, 13.3 us)
Async XLA Ops:
  7.2 4.5 copy-start
  7.2 93.6 %all-gather.2.cloned.1.call-start = ((), (), s32[]{:S(2)}) async-start(), calls=%async_computation.2 | async-start | bytes 8519680 | tf_op jit(solution)/shard_map/all_gather | solution.py:145
  11.7 1.4 copy-start.25
  11.7 2.0 copy-start.35
  11.7 3.0 copy-start.30
  13.1 36.1 %copy-start.13 = (bf16[256,12,256]{2,0,1:T(8,128)(2,1)S(1)}, bf16[256,12,256]{2,0,1:T(8,128)(2,1)}, u32[]{:S(2)}) copy-start(bf16[256,12,256]{2,0,1:T(8,128)(2,1)} %param.14) | copy-start | bytes 4718596
  14.7 30.9 %copy-start.4 = (bf16[256,256]{1,0:T(8,128)(2,1)S(1)}, bf16[256,256]{1,0:T(8,128)(2,1)}, u32[]{:S(2)}) copy-start(bf16[256,256]{1,0:T(8,128)(2,1)} %fusion.34) | copy-start | bytes 393220
  15.1 33.7 %copy-start.33 = (s32[32,1]{0,1:T(1,128)}, s32[32,1]{0,1:T(1,128)S(1)}, u32[]{:S(2)}) copy-start(s32[32,1]{0,1:T(1,128)S(1)} %get-tuple-element.15) | copy-start | bytes 388
  15.2 19.9 %copy-start.28 = (s32[128]{0:T(128)}, s32[128]{0:T(128)S(1)}, u32[]{:S(2)}) copy-start(s32[128]{0:T(128)S(1)} %get-tuple-element.11) | copy-start | bytes 1540
  15.2 33.6 %copy-start.31 = (s32[128]{0:T(128)}, s32[128]{0:T(128)S(1)}, u32[]{:S(2)}) copy-start(s32[128]{0:T(128)S(1)} %get-tuple-element.10) | copy-start | bytes 1540
  16.0 133.7 %all-to-all-start = ((s32[64,1,2]{2,1,0:T(1,128)}), s32[64,1,2]{2,1,0:T(1,128)}, u32[]{:S(2)}, u32[]{:S(2)}) async-start(s32[64,1,2]{2,1,0:T(1,128)} %bitcast.38), calls=%async_computation | async-start | bytes 65536 | tf_op jit(solution)/shard_map/all_to_all | solution.py:140
  48.9 10.1 %copy-start.24 = (bf16[244,256]{1,0:T(8,128)(2,1)S(1)}, bf16[244,256]{1,0:T(8,128)(2,1)}, u32[]{:S(2)}) copy-start(bf16[244,256]{1,0:T(8,128)(2,1)} %slice.139) | copy-start | bytes 374788
  59.1 3.5 copy-start.12
  59.1 2.0 copy-start.37
  62.5 1.7 copy-start.10
  64.2 1.2 copy-start.6
  65.4 4.8 copy-start.34
  65.4 4.8 copy-start.32
  65.4 4.8 copy-start.29
  65.4 4.9 %copy-start.36 = (pred[8,4]{0,1:T(4,128)(4,1)S(1)}, pred[8,4]{0,1:T(4,128)(4,1)}, u32[]{:S(2)}) copy-start(pred[8,4]{0,1:T(4,128)(4,1)} %copy.47) | copy-start | bytes 100
  65.4 4.9 %copy-start.26 = (s32[64,2]{1,0:T(8,128)S(1)}, s32[64,2]{1,0:T(8,128)}, u32[]{:S(2)}) copy-start(s32[64,2]{1,0:T(8,128)} %reduce_sum.109) | copy-start | bytes 1540
  70.2 55.9 %copy-start.8 = (bf16[8,384,256]{2,1,0:T(8,128)(2,1)}, bf16[8,384,256]{2,1,0:T(8,128)(2,1)S(1)}, u32[]{:S(2)}) copy-start(bf16[8,384,256]{2,1,0:T(8,128)(2,1)S(1)} %reshape.248) | copy-start | bytes 4718596
  126.1 3.8 copy-start.5
  130.4 3.8 copy-start.9
  134.2 1.7 copy-start.2
  135.9 6.4 %copy-start.27 = (pred[64,2]{1,0:T(8,128)(4,1)S(1)}, pred[64,2]{1,0:T(8,128)(4,1)}, u32[]{:S(2)}) copy-start(pred[64,2]{1,0:T(8,128)(4,1)} %broadcast_in_dim.116) | copy-start | bytes 388
  149.7 9.1 %copy-start.3 = (bf16[8,384,512]{2,1,0:T(8,128)(2,1)S(1)}, bf16[8,384,512]{2,1,0:T(8,128)(2,1)}, u32[]{:S(2)}) copy-start(bf16[8,384,512]{2,1,0:T(8,128)(2,1)} %copy-done.2) | copy-start | bytes 9437188
  149.7 308.8 %all-to-all-start.1 = ((bf16[64,2,128,256]{3,2,1,0:T(8,128)(2,1)}), bf16[64,2,128,256]{3,2,1,0:T(8,128)(2,1)}, u32[]{:S(2)}, u32[]{:S(2)}) async-start(bf16[64,2,128,256]{3,2,1,0:T(8,128)(2,1)} %select_select_fusion), calls=%async_computation.1 | async-start | bytes 16777216 | tf_op jit(solution)/shard_map/all_to_all | solution.py:159
  156.6 293.7 %all-reduce.28.cloned.1.call-start = ((), (), s32[]{:S(2)}) async-start(), calls=%async_computation.3 | async-start | bytes 6291456 | tf_op jit(solution)/shard_map/psum | solution.py:169
  163.0 4.8 copy-start.11
  191.4 2.3 copy-start.7
  470.8 5.0 %copy-start.14 = (f32[249,256]{1,0:T(8,128)S(1)}, f32[249,256]{1,0:T(8,128)}, u32[]{:S(2)}) copy-start(f32[249,256]{1,0:T(8,128)} %slice_bitcast_fusion) | copy-start | bytes 764932
  470.8 5.1 %copy-start.15 = (f32[250,256]{1,0:T(8,128)S(1)}, f32[250,256]{1,0:T(8,128)}, u32[]{:S(2)}) copy-start(f32[250,256]{1,0:T(8,128)} %slice_bitcast_fusion.1) | copy-start | bytes 768004
  470.8 5.1 %copy-start.16 = (f32[251,256]{1,0:T(8,128)S(1)}, f32[251,256]{1,0:T(8,128)}, u32[]{:S(2)}) copy-start(f32[251,256]{1,0:T(8,128)} %slice_bitcast_fusion.2) | copy-start | bytes 771076
  470.8 5.1 %copy-start.17 = (f32[252,256]{1,0:T(8,128)S(1)}, f32[252,256]{1,0:T(8,128)}, u32[]{:S(2)}) copy-start(f32[252,256]{1,0:T(8,128)} %slice_bitcast_fusion.3) | copy-start | bytes 774148
  470.8 5.1 %copy-start.18 = (f32[253,256]{1,0:T(8,128)S(1)}, f32[253,256]{1,0:T(8,128)}, u32[]{:S(2)}) copy-start(f32[253,256]{1,0:T(8,128)} %slice_bitcast_fusion.4) | copy-start | bytes 777220
  470.8 5.1 %copy-start.19 = (f32[254,256]{1,0:T(8,128)S(1)}, f32[254,256]{1,0:T(8,128)}, u32[]{:S(2)}) copy-start(f32[254,256]{1,0:T(8,128)} %slice_bitcast_fusion.5) | copy-start | bytes 780292
  470.9 5.1 %copy-start.20 = (f32[255,256]{1,0:T(8,128)S(1)}, f32[255,256]{1,0:T(8,128)}, u32[]{:S(2)}) copy-start(f32[255,256]{1,0:T(8,128)} %slice_bitcast_fusion.6) | copy-start | bytes 783364
  470.9 5.1 %copy-start.21 = (f32[244,256]{1,0:T(8,128)S(1)}, f32[244,256]{1,0:T(8,128)}, u32[]{:S(2)}) copy-start(f32[244,256]{1,0:T(8,128)} %slice_bitcast_fusion.7) | copy-start | bytes 749572
  470.9 5.1 %copy-start.22 = (f32[245,256]{1,0:T(8,128)S(1)}, f32[245,256]{1,0:T(8,128)}, u32[]{:S(2)}) copy-start(f32[245,256]{1,0:T(8,128)} %slice_bitcast_fusion.8) | copy-start | bytes 752644
  470.9 5.1 %copy-start.23 = (f32[246,256]{1,0:T(8,128)S(1)}, f32[246,256]{1,0:T(8,128)}, u32[]{:S(2)}) copy-start(f32[246,256]{1,0:T(8,128)} %slice_bitcast_fusion.9) | copy-start | bytes 755716
  470.9 7.2 %copy-start.1 = (bf16[512,256]{1,0:T(8,128)(2,1)S(1)}, bf16[512,256]{1,0:T(8,128)(2,1)}, u32[]{:S(2)}) copy-start(bf16[512,256]{1,0:T(8,128)(2,1)} %param.10) | copy-start | bytes 786436
Sparse Core Ops, SparseCore 0:
  14.9 85.8 all-gather.1
  193.8 256.3 all-reduce.27
where the time goes:
time: 491 us; the launch traced here: 485 us
  waiting for transfers between devices  278 us (57%)
  local copies, waits for them, and re-layouts  95.8 us (20%)
  other arithmetic  52.4 us (11%)
  matrix products  24.5 us (5%)
  starting transfers between devices  19.6 us (4%)
  between operations  15.1 us (3%)
    psum x1, waiting for transfers between devices, local(): head_total = lax.psum(head_part, 'dp')  247 us
    all_gather x1, waiting for transfers between devices, local(): segment = lax.all_gather(target, 'dp', axis=0, tiled=True)  30.4 us
    unnamed x91, local copies, waits for them, and re-layouts  28.1 us
    mul x1, other arithmetic, score_piece(): unit_pred * radial  21.8 us
    slice x12, local copies, waits for them, and re-layouts, score_piece(): target[step_index + 1:]  17.5 us
    all_to_all x1, starting transfers between devices, local(): lax.all_to_all(wanted, 'dp', split_axis=0, concat_axis=0, tiled=True)  12.7 us
    gather x2, local copies, waits for them, and re-layouts, local(): jnp.take_along_axis(segment_blocks, wanted[:, :, None, None], axis=1)  10.7 us
  transfers between devices with their start and end apart: 4, of which 2 were waited for; matrix products, arithmetic and copies ran while one was open for 29% of the time, Pallas kernels for 0%

commit v1 on v0

--- a/solution.py
+++ b/solution.py
@@ -142,7 +142,9 @@
         ecg.reshape(-1), conv_first, conv_second, conv_third, enc_gain, ctx_weight
     )
     positions, channels = target.shape
-    segment = lax.all_gather(target, "dp", axis=0, tiled=True)
+    segment = jnp.concatenate(
+        lax.all_to_all(jnp.stack([target] * lax.axis_size("dp")), "dp", 0, 0), axis=0
+    )
     piece_count = segment.shape[0] // positions
     segment_blocks = segment.reshape(piece_count, positions // 128, 128, channels)
     chosen = jnp.take_along_axis(segment_blocks, wanted[:, :, None, None], axis=1)

time: 491 us -> 619 us (1.26)
  waiting for transfers between devices: 278 us -> 404 us
  starting transfers between devices: 19.6 us -> 30.6 us
  local copies, waits for them, and re-layouts: 95.8 us -> 88.2 us
    all_to_all x0 -> x1, waiting for transfers between devices: none -> 155 us  [local(): lax.all_to_all(jnp.stack([target] * lax.axis_size('dp')), 'dp', 0, 0)]
    all_gather x1 -> x0, waiting for transfers between devices: 30.4 us -> none  [local(): segment = lax.all_gather(target, 'dp', axis=0, tiled=True)]
    all_to_all x0 -> x1, starting transfers between devices: none -> 12.6 us  [local(): lax.all_to_all(jnp.stack([target] * lax.axis_size('dp')), 'dp', 0, 0)]
    slice x12 -> x13, local copies, waits for them, and re-layouts: 17.5 us -> 6.85 us  [score_piece(): target[step_index + 1:]]
    unnamed x91 -> x73, local copies, waits for them, and re-layouts: 28.1 us -> 27.1 us
  transfers between devices with their start and end apart: 4 -> 4, of which waited for: 2 -> 2; matrix products, arithmetic and copies ran while one was open for 29% -> 21% of each run, Pallas kernels for 0% -> 0%
where the time goes in v1:
time: 619 us; the launch traced here: 613 us
  waiting for transfers between devices  404 us (65%)
  local copies, waits for them, and re-layouts  88.2 us (14%)
  other arithmetic  50.8 us (8%)
  starting transfers between devices  30.6 us (5%)
  matrix products  24.5 us (4%)
  between operations  15 us (2%)
    psum x1, waiting for transfers between devices, local(): head_total = lax.psum(head_part, 'dp')  249 us
    all_to_all x1, waiting for transfers between devices, local(): lax.all_to_all(jnp.stack([target] * lax.axis_size('dp')), 'dp', 0, 0)  155 us
    unnamed x73, local copies, waits for them, and re-layouts  27.1 us
    mul x1, other arithmetic, score_piece(): unit_pred * radial  21.9 us
    all_to_all x1, starting transfers between devices, local(): lax.all_to_all(jnp.stack([target] * lax.axis_size('dp')), 'dp', 0, 0)  12.6 us
  transfers between devices with their start and end apart: 4, of which 2 were waited for; matrix products, arithmetic and copies ran while one was open for 21% of the time, Pallas kernels for 0%

profile of v1, /device:TPU:8, one launch (start us, length us, event | category | flops | bytes accessed | tf_op | source)
XLA Modules:
  0.0 612.6 jit_solution(872492545052850425)
XLA Ops:
  7.2 0.8 reduce
  8.4 3.0 fusion.12
  11.7 1.3 fusion.22
  14.0 4.2 stack.41
  18.2 12.6 %all-to-all-start = ((bf16[64,256,256]{2,1,0:T(8,128)(2,1)}), bf16[64,256,256]{2,1,0:T(8,128)(2,1)}, u32[]{:S(2)}, u32[]{:S(2)}) async-start(bf16[64,256,256]{2,1,0:T(8,128)(2,1)} %stack.41), calls=%async_computation | async-start | bytes 16777216 | tf_op jit(solution)/shard_map/all_to_all | solution.py:146
  30.9 0.7 slice.128
  31.6 0.7 slice.129
  38.2 0.7 broadcast_in_dim_reshape.2
  39.0 0.7 all_to_all.13
  39.7 0.7 copy.44
  40.4 0.9 bitcast_dynamic-update-slice_fusion.11
  41.3 0.9 bitcast_dynamic-update-slice_fusion.10
  42.2 0.9 bitcast_dynamic-update-slice_fusion.9
  43.2 0.9 bitcast_dynamic-update-slice_fusion.8
  44.1 0.9 bitcast_dynamic-update-slice_fusion.7
  45.0 0.9 bitcast_dynamic-update-slice_fusion.6
  46.0 0.9 bitcast_dynamic-update-slice_fusion.3
  46.9 0.9 bitcast_dynamic-update-slice_fusion.2
  47.8 0.9 bitcast_dynamic-update-slice_fusion.1
  48.7 0.9 bitcast_dynamic-update-slice_fusion
  49.7 1.9 fusion.32
  51.6 0.7 fusion.40
  52.3 0.7 multiply_reduce_fusion.1
  53.1 1.2 fusion.2
  54.8 1.2 copy-done.6
  56.0 2.3 copy.45
  58.3 2.5 reshape.247
  62.0 155.0 %all-to-all-done = bf16[64,256,256]{2,1,0:T(8,128)(2,1)} async-done(((bf16[64,256,256]{2,1,0:T(8,128)(2,1)}), bf16[64,256,256]{2,1,0:T(8,128)(2,1)}, u32[]{:S(2)}, u32[]{:S(2)}) %all-to-all-start) | async-done | bytes 8388640 | tf_op jit(solution)/shard_map/all_to_all | solution.py:146
  217.0 6.8 %all-to-all-start.1 = ((s32[64,1,2]{2,1,0:T(1,128)}), s32[64,1,2]{2,1,0:T(1,128)S(1)}, u32[]{:S(2)}, u32[]{:S(2)}) async-start(s32[64,1,2]{2,1,0:T(1,128)} %bitcast.38), calls=%async_computation.1 | async-start | bytes 65536 | tf_op jit(solution)/shard_map/all_to_all | solution.py:140
  223.8 10.6 %gather_fusion.2 = bf16[128,128,256]{2,1,0:T(8,128)(2,1)} fusion(bf16[64,2,128,256]{3,2,1,0:T(8,128)(2,1)} %bitcast.23, s32[128]{0:T(128)S(1)} %reshape.271), kind=kCustom, calls=%fused_computation.2 | custom fusion | bytes 16778240 | tf_op jit(solution)/shard_map/jit(take_along_axis)/gather | solution.py:150
  234.4 7.4 %broadcast_select_fusion = bf16[128,128,256]{2,1,0:T(8,128)(2,1)} fusion(bf16[128,128,256]{2,1,0:T(8,128)(2,1)} %gather_fusion.2, pred[128]{0:T(512)(128)(4,1)S(1)} %compare_and_fusion.1), kind=kLoop, calls=%fused_computation.5 | loop fusion | flops 4194304 | bytes 16777344 | tf_op jit(solution)/shard_map/jit(take_along_axis)/select_n | solution.py:150
  241.8 5.4 gather_fusion
  247.2 1.9 bitcast_select_fusion
  249.1 3.8 fusion.1
  253.4 3.6 divide_convert_fusion
  257.1 1.4 convolution_convert_fusion
  258.7 6.4 %gather_fusion.1 = bf16[128,128,256]{2,1,0:T(8,128)(2,1)} fusion(bf16[32,128,256]{2,1,0:T(8,128)(2,1)S(1)} %bitcast.125, s32[1024]{0:T(1024)S(1)} %get-tuple-element.28), kind=kCustom, calls=%fused_computation.1 | custom fusion | bytes 16777728 | tf_op jit(solution)/shard_map/jit(_take)/gather | solution.py:157
  265.1 7.4 %select_select_fusion = bf16[64,2,128,256]{3,2,1,0:T(8,128)(2,1)} fusion(bf16[64,2,128,256]{3,2,1,0:T(8,128)(2,1)} %bitcast.126, pred[64,2]{1,0:T(8,128)(4,1)S(1)} %compare_and_fusion, pred[64,2]{1,0:T(8,128)(4,1)S(1)} %broadcast_in_dim.116), kind=kLoop, calls=%fused_computation.4 | loop fusion | flops 8388608 | bytes 16777472 | tf_op jit(solution)/shard_map/jit(_where)/select_n | solution.py:158
  272.5 10.9 %all-to-all-start.2 = ((bf16[64,2,128,256]{3,2,1,0:T(8,128)(2,1)}), bf16[64,2,128,256]{3,2,1,0:T(8,128)(2,1)}, u32[]{:S(2)}, u32[]{:S(2)}) async-start(bf16[64,2,128,256]{3,2,1,0:T(8,128)(2,1)} %select_select_fusion), calls=%async_computation.2 | async-start | bytes 16777216 | tf_op jit(solution)/shard_map/all_to_all | solution.py:161
  284.2 0.7 reduce.8
  285.1 4.2 fusion.105
  289.3 4.8 reshape.252
  294.1 21.9 %divide_convert_fusion.1 = bf16[256,12,256]{2,0,1:T(8,128)(2,1)} fusion(f32[256,12]{0,1:T(8,128)S(1)} %add_sqrt_fusion, f32[256,12,256]{2,1,0:T(8,128)} %reshape.252, bf16[256,12,256]{2,0,1:T(8,128)(2,1)} %copy-done.12, f32[256,12]{0,1:T(8,128)S(1)} %get-tuple-element.18, f32[256,12,256]{2,0,1:T(8,128)S(1)} %copy-done.11), kind=kOutput, calls=%fused_computation.14 | output fusion | flops 10226943 | bytes 9461760 | tf_op jit(solution)/shard_map/mul | solution.py:111
  316.0 1.7 copy.53
  317.7 2.3 fusion.106
  320.5 0.7 slice_bitcast_fusion.10
  321.2 0.7 slice_bitcast_fusion.11
  322.0 0.7 slice_bitcast_fusion.7
  322.7 0.7 slice_bitcast_fusion.8
  323.4 0.7 slice_bitcast_fusion
  324.1 0.7 slice_bitcast_fusion.9
  324.8 0.7 slice_bitcast_fusion.1
  325.6 0.7 slice_bitcast_fusion.2
  326.3 0.7 slice_bitcast_fusion.3
  327.0 0.7 slice_bitcast_fusion.4
  327.7 0.7 slice_bitcast_fusion.5
  328.4 0.7 slice_bitcast_fusion.6
  329.1 248.6 %all-reduce.28.cloned.1.call-done = f32[256,3072]{1,0:T(8,128)} async-done(((f32[256,3072]{1,0:T(8,128)}), f32[256,3072]{1,0:T(8,128)}) %all-reduce.28.cloned.1.call-update) | async-done | bytes 3145744 | tf_op jit(solution)/shard_map/psum | solution.py:171
  577.7 2.1 broadcast_multiply_fusion
  579.9 2.4 copy.54
  582.2 3.7 copy.55
  586.0 12.3 %copy.58 = bf16[16,8,128,256]{3,1,2,0:T(8,128)(2,1)} copy(bf16[16,8,128,256]{3,2,1,0:T(8,128)(2,1)} %bitcast.52) | data formatting | bytes 16777216
  598.4 4.7 fusion.90
  603.5 2.1 multiply_bitcast_fusion
  (120 shorter events, 11.5 us)
Async XLA Ops:
  7.2 4.5 copy-start
  11.7 1.4 copy-start.24
  11.7 1.9 copy-start.27
  14.0 23.1 %copy-start.4 = (bf16[256,256]{1,0:T(8,128)(2,1)}, bf16[256,256]{1,0:T(8,128)(2,1)S(1)}, u32[]{:S(2)}) copy-start(bf16[256,256]{1,0:T(8,128)(2,1)S(1)} %fusion.34) | copy-start | bytes 393220
  18.2 19.5 %copy-start.26 = (s32[1,8,4,2]{1,3,2,0:T(2,128)S(1)}, s32[1,8,4,2]{1,3,2,0:T(2,128)}, u32[]{:S(2)}) copy-start(s32[1,8,4,2]{1,3,2,0:T(2,128)} %param.15) | copy-start | bytes 772
  18.2 198.7 %all-to-all-start = ((bf16[64,256,256]{2,1,0:T(8,128)(2,1)}), bf16[64,256,256]{2,1,0:T(8,128)(2,1)}, u32[]{:S(2)}, u32[]{:S(2)}) async-start(bf16[64,256,256]{2,1,0:T(8,128)(2,1)} %stack.41), calls=%async_computation | async-start | bytes 16777216 | tf_op jit(solution)/shard_map/all_to_all | solution.py:146
  30.9 8.8 %copy-start.13 = (bf16[256,12,256]{2,0,1:T(8,128)(2,1)S(1)}, bf16[256,12,256]{2,0,1:T(8,128)(2,1)}, u32[]{:S(2)}) copy-start(bf16[256,12,256]{2,0,1:T(8,128)(2,1)} %param.14) | copy-start | bytes 4718596
  37.7 8.2 %slice-start = ((bf16[256,256]{1,0:T(8,128)(2,1)}), bf16[248,256]{1,0:T(8,128)(2,1)S(1)}, s32[]{:S(2)}) async-start(bf16[256,256]{1,0:T(8,128)(2,1)} %copy-done.4), calls=%async_computation.4 | async-start | bytes 253952 | tf_op jit(solution)/shard_map/slice | solution.py:66
  49.6 3.5 copy-start.12
  49.6 2.0 copy-start.28
  53.1 1.7 copy-start.10
  54.8 1.2 copy-start.6
  56.0 4.7 copy-start.25
  60.8 188.4 %copy-start.8 = (bf16[8,384,256]{2,1,0:T(8,128)(2,1)}, bf16[8,384,256]{2,1,0:T(8,128)(2,1)S(1)}, u32[]{:S(2)}) copy-start(bf16[8,384,256]{2,1,0:T(8,128)(2,1)S(1)} %reshape.247) | copy-start | bytes 4718596
  217.0 55.6 %all-to-all-start.1 = ((s32[64,1,2]{2,1,0:T(1,128)}), s32[64,1,2]{2,1,0:T(1,128)S(1)}, u32[]{:S(2)}, u32[]{:S(2)}) async-start(s32[64,1,2]{2,1,0:T(1,128)} %bitcast.38), calls=%async_computation.1 | async-start | bytes 65536 | tf_op jit(solution)/shard_map/all_to_all | solution.py:140
  249.1 3.8 copy-start.5
  253.4 3.6 copy-start.9
  257.1 1.7 copy-start.2
  272.5 12.6 %copy-start.3 = (bf16[8,384,512]{2,1,0:T(8,128)(2,1)S(1)}, bf16[8,384,512]{2,1,0:T(8,128)(2,1)}, u32[]{:S(2)}) copy-start(bf16[8,384,512]{2,1,0:T(8,128)(2,1)} %copy-done.2) | copy-start | bytes 9437188
  272.5 313.4 %all-to-all-start.2 = ((bf16[64,2,128,256]{3,2,1,0:T(8,128)(2,1)}), bf16[64,2,128,256]{3,2,1,0:T(8,128)(2,1)}, u32[]{:S(2)}, u32[]{:S(2)}) async-start(bf16[64,2,128,256]{3,2,1,0:T(8,128)(2,1)} %select_select_fusion), calls=%async_computation.2 | async-start | bytes 16777216 | tf_op jit(solution)/shard_map/all_to_all | solution.py:161
  283.5 294.3 %all-reduce.28.cloned.1.call-start = ((), (), s32[]{:S(2)}) async-start(), calls=%async_computation.3 | async-start | bytes 6291456 | tf_op jit(solution)/shard_map/psum | solution.py:171
  289.3 4.8 copy-start.11
  317.7 2.3 copy-start.7
  598.3 5.0 copy-start.14
  598.3 5.1 copy-start.15
  598.3 5.1 copy-start.16
  598.3 5.1 copy-start.17
  598.3 5.1 copy-start.18
  598.3 5.1 copy-start.19
  598.3 5.1 copy-start.20
  598.3 5.1 copy-start.21
  598.4 5.1 copy-start.22
  598.4 5.1 copy-start.23
  598.4 7.2 %copy-start.1 = (bf16[512,256]{1,0:T(8,128)(2,1)S(1)}, bf16[512,256]{1,0:T(8,128)(2,1)}, u32[]{:S(2)}) copy-start(bf16[512,256]{1,0:T(8,128)(2,1)} %param.10) | copy-start | bytes 786436
Sparse Core Ops, SparseCore 0:
  320.1 257.5 all-reduce.27
